TPU v7x, 32 devices: a whole 2x2x4 slice. The times are simulated.
32 devices in a mesh: dp: 4 (over x, core), seq: 2 (over y), fsdp: 4 (over z).
Axes of the slice: x: 2, y: 2, z: 4, core: 2. Of those that a mesh axis runs over, the one named last changes fastest.
Arguments:
- tokens: bfloat16 [16, 1536, 768], P(('dp', 'fsdp'), 'seq'), may hold values from -6 to 6
- attn_in: bfloat16 [768, 2304], P('fsdp'), may hold values from -0.21875 to 0.21875
- attn_out: bfloat16 [768, 768], P('fsdp'), may hold values from -1.75 to 1.75
- router: bfloat16 [768, 4], P('fsdp'), may hold values from -0.15625 to 0.15625
- gains: bfloat16 [768, 2], P('fsdp'), may hold values from 0.5 to 1.5
- expert_w: bfloat16 [3072, 4, 1536], P('fsdp'), may hold values from -0.21875 to 0.21875
- expert_ids: int32 [16, 1536, 2], P(('dp', 'fsdp'), 'seq'), may hold values from 0 to 3, all different within a row
- segments: int32 [16, 512], P(('dp', 'fsdp')), may hold values from 0 to 1, as said below
- cotangent: bfloat16 [16, 1536, 768], P(('dp', 'fsdp'), 'seq'), may hold values from -6 to 6
Outputs:
- block_out: bfloat16 [16, 1536, 768], P(('dp', 'fsdp'), 'seq')
- d_tokens: bfloat16 [16, 1536, 768], P(('dp', 'fsdp'), 'seq')
- d_attn_in: float32 [768, 2304], P('fsdp')
- d_attn_out: float32 [768, 768], P('fsdp')
- d_router: float32 [768, 4], P('fsdp')
- d_gains: float32 [768, 2], P('fsdp')
- d_expert: float32 [3072, 4, 1536], P('fsdp')
Inputs may be any that keep to these rules, and one draw needn't show every extreme that they name: `expert_ids`: the two experts of a token differ. `segments`: never falls along a group; every continuation has 64 to 384 tokens, and in every group one has exactly 384.
All inputs are finite; a program needn't handle non-finite values.
Results may differ from a plain program's by a relative error of at most 0.018.
Values may be sent and summed in bfloat16 or wider, within the bound.
A program may use at most 384 MiB of HBM per device.

v0:
```python
import jax
import jax.numpy as jnp
from jax import lax
from jax.sharding import PartitionSpec as P

HEADS = 12
HEAD_DIM = 64
EXPERTS = 4
PROMPT = 1024
EPSILON = 1e-06
NEGATIVE = -1e30
HIGH = lax.Precision.HIGHEST


def route(choose, capacity, experts_count):
    pair_expert = choose.reshape(-1)
    one_hot = (pair_expert[:, None] == jnp.arange(experts_count, dtype=jnp.int32)[None, :]).astype(
        jnp.int32
    )
    before = jnp.cumsum(one_hot, axis=0) - one_hot
    place = jnp.sum(before * one_hot, axis=1)
    kept = place < capacity
    slots = jnp.where(kept, pair_expert * capacity + place, experts_count * capacity)
    pair_count = pair_expert.shape[0]
    pair_of = (
        jnp.zeros((experts_count * capacity + 1,), jnp.int32)
        .at[slots]
        .set(jnp.arange(pair_count, dtype=jnp.int32))
    )
    filled = (
        jnp.zeros((experts_count * capacity + 1,), jnp.int32)
        .at[slots]
        .set(jnp.ones((pair_count,), jnp.int32))
    )
    return (slots, kept, pair_of[:-1], filled[:-1] > 0)


def expert_pre(expert_in, piece):
    width = piece.shape[2] // 2
    return jnp.einsum(
        "ecd,fed->ecf", expert_in, piece[:, :, :width], preferred_element_type=jnp.float32
    )


def expert_out(activity, piece):
    width = piece.shape[2] // 2
    return jnp.einsum(
        "ecf,fed->ecd", activity, piece[:, :, width:], preferred_element_type=jnp.float32
    )


def expert_back(grad_result, pre_rows, piece):
    width = piece.shape[2] // 2
    grad_act = jnp.einsum(
        "ecd,fed->ecf", grad_result, piece[:, :, width:], preferred_element_type=jnp.float32
    )
    grad_pre = jax.vjp(jax.nn.gelu, pre_rows)[1](grad_act)[0].astype(jnp.bfloat16)
    grad_in = jnp.einsum(
        "ecf,fed->ecd", grad_pre, piece[:, :, :width], preferred_element_type=jnp.float32
    )
    return (grad_pre, grad_in)


def shards(tokens, attn_in, attn_out, router, gains, expert_w, expert_ids, segments, cotangent):
    x_rows = tokens[0].astype(jnp.float32)
    tok_rows = x_rows.shape[0]
    width = x_rows.shape[1]
    seq_count = lax.axis_size("seq")
    scale = HEAD_DIM ** (-0.5)
    w_qkv, w_proj, w_route, gain_pair = (
        lax.all_gather(attn_in, "fsdp", axis=0, tiled=True),
        lax.all_gather(attn_out, "fsdp", axis=0, tiled=True),
        lax.all_gather(router, "fsdp", axis=0, tiled=True),
        lax.all_gather(gains, "fsdp", axis=0, tiled=True),
    )
    gain_f = gain_pair.astype(jnp.float32)
    r_one = lax.rsqrt(jnp.mean(x_rows * x_rows, axis=-1, keepdims=True) + EPSILON)
    normed_one = x_rows * r_one
    normed_low = (normed_one * gain_f[:, 0]).astype(jnp.bfloat16)
    projected = jnp.dot(normed_low, w_qkv, preferred_element_type=jnp.float32).astype(jnp.bfloat16)
    local_heads = HEADS // seq_count
    head_cols = local_heads * HEAD_DIM
    arrived = lax.all_to_all(
        projected.reshape(tok_rows, 3, seq_count, head_cols),
        "seq",
        split_axis=2,
        concat_axis=0,
        tiled=True,
    )
    group_len = arrived.shape[0]
    queries = arrived[:, 0, 0].reshape(group_len, local_heads, HEAD_DIM)
    keys = arrived[:, 1, 0].reshape(group_len, local_heads, HEAD_DIM)
    values = arrived[:, 2, 0].reshape(group_len, local_heads, HEAD_DIM)
    seg_full = jnp.concatenate([jnp.full((PROMPT,), -1, jnp.int32), segments[0]])
    block = min(512, group_len)
    key_place = jnp.arange(group_len, dtype=jnp.int32)
    begins = jnp.arange(group_len // block, dtype=jnp.int32) * block

    def block_scores(begin):
        query_block = lax.dynamic_slice_in_dim(queries, begin, block, 0)
        query_place = begin + jnp.arange(block, dtype=jnp.int32)
        query_seg = lax.dynamic_slice_in_dim(seg_full, begin, block, 0)
        raw = (
            jnp.einsum("qhd,khd->hqk", query_block, keys, preferred_element_type=jnp.float32)
            * scale
        )
        allowed = (key_place[None, :] <= query_place[:, None]) & (
            (seg_full[None, :] < 0) | (seg_full[None, :] == query_seg[:, None])
        )
        return (jnp.where(allowed[None], raw, NEGATIVE), query_block)

    def forward_block(begin):
        masked, query_block = block_scores(begin)
        row_max = jnp.max(masked, axis=-1, keepdims=True)
        expo = jnp.exp(masked - row_max)
        row_total = jnp.sum(expo, axis=-1, keepdims=True)
        probs = expo / row_total
        mixed_block = jnp.einsum(
            "hqk,khd->qhd", probs.astype(jnp.bfloat16), values, preferred_element_type=jnp.float32
        )
        return (mixed_block.astype(jnp.bfloat16), (row_max + jnp.log(row_total))[:, :, 0])

    mixed_blocks, log_totals = lax.map(forward_block, begins)
    mixed_heads = mixed_blocks.reshape(group_len, 1, head_cols)
    returned = lax.all_to_all(mixed_heads, "seq", split_axis=0, concat_axis=1, tiled=True)
    attended = returned.reshape(tok_rows, width)
    hidden = x_rows + jnp.dot(attended, w_proj, preferred_element_type=jnp.float32)
    r_two = lax.rsqrt(jnp.mean(hidden * hidden, axis=-1, keepdims=True) + EPSILON)
    normed_two = hidden * r_two
    routed_low = (normed_two * gain_f[:, 1]).astype(jnp.bfloat16)
    logits = jnp.dot(routed_low, w_route, preferred_element_type=jnp.float32)
    probs_r = jax.nn.softmax(logits, axis=-1)
    choose = expert_ids[0]
    choose_map = (choose[:, :, None] == jnp.arange(EXPERTS, dtype=jnp.int32)[None, None, :]).astype(
        jnp.float32
    )
    gates = jnp.sum(probs_r[:, None, :] * choose_map, axis=-1)
    capacity = 2 * tok_rows // EXPERTS
    slots, kept, pair_of, filled = route(choose, capacity, EXPERTS)
    token_of = pair_of // 2
    expert_in = jnp.where(
        filled[:, None], routed_low[token_of], jnp.zeros((), jnp.bfloat16)
    ).reshape(EXPERTS, capacity, width)
    piece = lax.all_gather(expert_w, "fsdp", axis=0, tiled=True)
    pre_rows = expert_pre(expert_in, piece)
    result = expert_out(jax.nn.gelu(pre_rows).astype(jnp.bfloat16), piece)
    padded = jnp.concatenate(
        [result.reshape(EXPERTS * capacity, width), jnp.zeros((1, width), jnp.float32)], axis=0
    )
    picked = padded[slots].reshape(tok_rows, 2, width)
    kept_f = kept.astype(jnp.float32).reshape(tok_rows, 2)
    weight_pair = gates * kept_f
    block_out = hidden + jnp.sum(weight_pair[..., None] * picked, axis=1)
    grad_out_rows = cotangent[0].astype(jnp.float32)
    grad_gates = kept_f * jnp.sum(grad_out_rows[:, None, :] * picked, axis=-1)
    grad_probs = jnp.sum(grad_gates[:, :, None] * choose_map, axis=1)
    grad_logits = probs_r * (grad_probs - jnp.sum(probs_r * grad_probs, axis=-1, keepdims=True))
    grad_route_w = jnp.dot(routed_low.astype(jnp.float32).T, grad_logits, precision=HIGH)
    grad_routed = jnp.dot(grad_logits, w_route.astype(jnp.float32).T, precision=HIGH)
    scaled = (weight_pair[:, :, None] * grad_out_rows[:, None, :]).reshape(2 * tok_rows, width)
    grad_result = (
        jnp.where(filled[:, None], scaled[pair_of], 0.0)
        .astype(jnp.bfloat16)
        .reshape(EXPERTS, capacity, width)
    )
    piece = lax.all_gather(expert_w, "fsdp", axis=0, tiled=True)
    pre_rows = expert_pre(expert_in, piece)
    act_rows = jax.nn.gelu(pre_rows).astype(jnp.bfloat16)
    grad_pre_rows, grad_in_rows = expert_back(grad_result, pre_rows, piece)
    act_store = act_rows
    pre_rows = grad_pre_rows
    act_rows = act_store
    grad_first = jnp.einsum("ecd,ecf->fed", expert_in, pre_rows, preferred_element_type=jnp.float32)
    grad_second = jnp.einsum(
        "ecf,ecd->fed", act_rows, grad_result, preferred_element_type=jnp.float32
    )
    expert_shard = lax.psum_scatter(
        jnp.concatenate([grad_first, grad_second], axis=2).astype(jnp.bfloat16),
        "fsdp",
        scatter_dimension=0,
        tiled=True,
    )
    padded_in = jnp.concatenate(
        [grad_in_rows.reshape(EXPERTS * capacity, width), jnp.zeros((1, width), jnp.float32)],
        axis=0,
    )
    grad_routed = grad_routed + jnp.sum(padded_in[slots].reshape(tok_rows, 2, width), axis=1)
    grad_gain_two = jnp.sum(grad_routed * normed_two, axis=0)
    scaled_two = grad_routed * gain_f[:, 1]
    grad_hidden = grad_out_rows + r_two * (
        scaled_two - normed_two * jnp.mean(scaled_two * normed_two, axis=-1, keepdims=True)
    )
    hid_low = grad_hidden.astype(jnp.bfloat16)
    grad_proj_w = jnp.dot(attended.T, hid_low, preferred_element_type=jnp.float32)
    grad_attended = jnp.dot(hid_low, w_proj.T, preferred_element_type=jnp.float32).astype(
        jnp.bfloat16
    )
    grad_heads = lax.all_to_all(
        grad_attended.reshape(tok_rows, seq_count, head_cols),
        "seq",
        split_axis=1,
        concat_axis=0,
        tiled=True,
    )
    grad_mixed = grad_heads.reshape(group_len, local_heads, HEAD_DIM)

    def back_block(carry, inputs):
        begin, log_rows = inputs
        masked, query_block = block_scores(begin)
        probs = jnp.exp(masked - log_rows[:, :, None])
        grad_block = lax.dynamic_slice_in_dim(grad_mixed, begin, block, 0)
        grad_p = jnp.einsum("qhd,khd->hqk", grad_block, values, preferred_element_type=jnp.float32)
        inner = jnp.sum(probs * grad_p, axis=-1, keepdims=True)
        grad_scores = (probs * (grad_p - inner)).astype(jnp.bfloat16)
        grad_query = (
            jnp.einsum("hqk,khd->qhd", grad_scores, keys, preferred_element_type=jnp.float32)
            * scale
        )
        grad_key = (
            carry[0]
            + jnp.einsum(
                "hqk,qhd->khd", grad_scores, query_block, preferred_element_type=jnp.float32
            )
            * scale
        )
        grad_value = carry[1] + jnp.einsum(
            "hqk,qhd->khd",
            probs.astype(jnp.bfloat16),
            grad_block,
            preferred_element_type=jnp.float32,
        )
        return ((grad_key, grad_value), grad_query)

    zero_heads = jnp.zeros((group_len, local_heads, HEAD_DIM), jnp.float32)
    (grad_keys, grad_values), grad_queries = lax.scan(
        back_block, (zero_heads, zero_heads), (begins, log_totals)
    )
    stacked = jnp.stack(
        [
            grad_queries.reshape(group_len, head_cols),
            grad_keys.reshape(group_len, head_cols),
            grad_values.reshape(group_len, head_cols),
        ],
        axis=1,
    )
    stacked = stacked.astype(jnp.bfloat16).reshape(group_len, 3, 1, head_cols)
    grad_back = lax.all_to_all(stacked, "seq", split_axis=0, concat_axis=2, tiled=True)
    grad_proj_rows = grad_back.reshape(tok_rows, 3 * width)
    grad_qkv_w = jnp.dot(normed_low.T, grad_proj_rows, preferred_element_type=jnp.float32)
    grad_normed = jnp.dot(grad_proj_rows, w_qkv.T, preferred_element_type=jnp.float32)
    grad_gain_one = jnp.sum(grad_normed * normed_one, axis=0)
    scaled_one = grad_normed * gain_f[:, 0]
    grad_x = grad_hidden + r_one * (
        scaled_one - normed_one * jnp.mean(scaled_one * normed_one, axis=-1, keepdims=True)
    )
    grad_gains = jnp.stack([grad_gain_one, grad_gain_two], axis=1)
    shard_qkv, shard_proj, shard_route, shard_gains = (
        lax.psum_scatter(
            grad_qkv_w.astype(jnp.bfloat16), "fsdp", scatter_dimension=0, tiled=True
        ).astype(jnp.float32),
        lax.psum_scatter(
            grad_proj_w.astype(jnp.bfloat16), "fsdp", scatter_dimension=0, tiled=True
        ).astype(jnp.float32),
        lax.psum_scatter(
            grad_route_w.astype(jnp.bfloat16), "fsdp", scatter_dimension=0, tiled=True
        ).astype(jnp.float32),
        lax.psum_scatter(
            grad_gains.astype(jnp.bfloat16), "fsdp", scatter_dimension=0, tiled=True
        ).astype(jnp.float32),
    )
    part_qkv, part_proj, part_expert = (
        lax.psum_scatter(
            shard_qkv.astype(jnp.bfloat16), ("dp", "seq"), scatter_dimension=1, tiled=True
        ).astype(jnp.float32),
        lax.psum_scatter(
            shard_proj.astype(jnp.bfloat16), ("dp", "seq"), scatter_dimension=1, tiled=True
        ).astype(jnp.float32),
        lax.psum_scatter(expert_shard, ("dp", "seq"), scatter_dimension=2, tiled=True).astype(
            jnp.float32
        ),
    )
    summed_qkv, summed_proj, summed_expert = (
        lax.all_gather(part_qkv.astype(jnp.bfloat16), ("dp", "seq"), axis=1, tiled=True).astype(
            part_qkv.dtype
        ),
        lax.all_gather(part_proj.astype(jnp.bfloat16), ("dp", "seq"), axis=1, tiled=True).astype(
            part_proj.dtype
        ),
        lax.all_gather(part_expert.astype(jnp.bfloat16), ("dp", "seq"), axis=2, tiled=True).astype(
            part_expert.dtype
        ),
    )
    summed_route, summed_gains = lax.psum((shard_route, shard_gains), ("dp", "seq"))
    return (
        block_out.astype(jnp.bfloat16)[None],
        grad_x.astype(jnp.bfloat16)[None],
        summed_qkv,
        summed_proj,
        summed_route,
        summed_gains,
        summed_expert,
    )


def solution(mesh):
    in_specs = (
        P(("dp", "fsdp"), "seq", None),
        P("fsdp", None),
        P("fsdp", None),
        P("fsdp", None),
        P("fsdp", None),
        P("fsdp", None, None),
        P(("dp", "fsdp"), "seq", None),
        P(("dp", "fsdp"), None),
        P(("dp", "fsdp"), "seq", None),
    )
    out_specs = (
        P(("dp", "fsdp"), "seq", None),
        P(("dp", "fsdp"), "seq", None),
        P("fsdp", None),
        P("fsdp", None),
        P("fsdp", None),
        P("fsdp", None),
        P("fsdp", None, None),
    )
    return jax.shard_map(shards, mesh=mesh, in_specs=in_specs, out_specs=out_specs, check_vma=False)
```

profile of v0, /device:TPU:0, one launch (start us, length us, event | category | flops | bytes accessed | tf_op | source)
XLA Modules:
  0.0 1859.5 jit_solution(3492848803113367879)
XLA Ops:
  8.7 9.3 copy.327
  18.7 13.0 all-gather
  33.3 49.0 %all-gather.7.cloned.1.call-done = bf16[768,2304]{1,0:T(8,128)(2,1)} async-done(((bf16[192,2304]{1,0:T(8,128)(2,1)}), bf16[768,2304]{1,0:T(8,128)(2,1)}) %all-gather.7.cloned.1.call-update) | async-done | bytes 3538960 | tf_op jit(solution)/shard_map/all_gather | solution.py:71
  82.3 6.6 convolution_convert_fusion.1
  88.9 6.5 reshape.438
  105.7 12.0 all-gather.1
  130.6 6.7 scatter_custom_fusion.1
  137.9 6.8 scatter_custom_fusion
  157.0 65.0 %while.28 = (s32[]{:T(128)}, bf16[3,512,6,64]{1,3,2,0:T(8,128)(2,1)}, f32[3,6,512]{2,1,0:T(8,128)}, s32[3]{0:T(128)S(1)}, s32[1536]{0:T(1024)S(1)}, /*index=5*/b...) while((s32[]{:T(128)}, ...), condition=%wide.region_4.5_spmd.clone, body=%wide.region_1.4_spmd.clone.sunk | while | flops 1267923968 | bytes 63042744 | solution.py:123
  170.9 7.1 fusion.155
  192.6 7.1 fusion.155
  214.2 7.1 fusion.155
  221.9 5.0 copy.357
  226.9 8.6 reshape.506
  236.0 10.1 reduce.12
  259.5 6.9 mul.300
  278.1 5.7 gather_fusion
  290.7 5.6 gather_fusion.2
  300.8 443.7 %all-gather.11.cloned.1.call-done = bf16[3072,4,1536]{2,0,1:T(8,128)(2,1)} async-done(((bf16[768,4,1536]{2,0,1:T(8,128)(2,1)}), bf16[3072,4,1536]{2,0,1:T(8,128)(2,1)}) %all-gather.11.cloned.1.call-update) | async-done | bytes 37748752 | tf_op jit(solution)/shard_map/all_gather | solution.py:144
  744.5 18.9 %fusion.56 = f32[4,384,3072]{2,1,0:T(8,128)} fusion(bf16[3072,4,1536]{2,0,1:T(8,128)(2,1)} %all-gather.11.cloned.1.call-done, bf16[4,384,768]{1,2,0:T(8,128)(2,1)S(1)} %copy-done.23, pred[4,384]{1,0:T(4,128)(4,1)S(1)} %copy-done.63), kind=kOutput, calls=%fused_computation.77 | convolution fusion | flops 7248936960 | bytes 40109568 | tf_op jit(solution)/shard_map/ecd,fed->ecf/dot_general | solution.py:40
  763.4 19.1 %convert_bitcast_fusion = bf16[3072,4,768]{0,2,1:T(8,128)(2,1)} fusion(bf16[4,384,768]{1,2,0:T(8,128)(2,1)S(1)} %copy-done.25, pred[4,384]{1,0:T(4,128)(4,1)S(1)} %copy-done.63, f32[4,384,3072]{2,1,0:T(8,128)} %fusion.56), kind=kOutput, calls=%fused_computation.68 | convolution fusion | flops 7300841472 | bytes 40109568 | tf_op jit(solution)/shard_map/ecf,ecd->fed/dot_general | solution.py:174
  782.5 25.0 %fusion.49 = bf16[4,384,3072]{2,1,0:T(8,128)(2,1)} fusion(f32[4,384,3072]{2,1,0:T(8,128)} %fusion.56, bf16[3072,4,1536]{2,0,1:T(8,128)(2,1)} %all-gather.11.cloned.1.call-done, bf16[4,384,768]{1,2,0:T(8,128)(2,1)} %copy.335, pred[4,384]{1,0:T(4,128)(4,1)S(1)} %copy-done.63), kind=kOutput, calls=%fused_computation.67 | convolution fusion | flops 7343308800 | bytes 49546752 | tf_op jit(solution)/shard_map/ecd,fed->ecf/dot_general | solution.py:54
  807.5 17.0 convert_bitcast_fusion.1
  824.5 25.8 %pad_maximum_fusion = bf16[3072,4,1536]{0,2,1:T(8,128)(2,1)} fusion(bf16[3072,4,768]{0,2,1:T(8,128)(2,1)} %convert_bitcast_fusion, bf16[3072,4,768]{0,2,1:T(8,128)(2,1)} %convert_bitcast_fusion.1), kind=kLoop, calls=%fused_computation.58 | loop fusion | flops 75497472 | bytes 75497472 | tf_op jit(solution)/shard_map/concatenate | solution.py:178
  851.8 18.4 fusion.52
  875.2 9.1 gather_fusion.1
  884.3 6.9 reshape.443
  891.2 13.5 multiply_reduce_fusion.1
  908.0 17.1 fusion.54
  929.9 9.1 gather_fusion.3
  939.0 6.9 reshape.445
  945.9 9.4 reduce_sum.159
  970.5 15.5 all-to-all-done.2
  994.5 176.0 %while.29 = (s32[]{:T(128)}, f32[1536,6,64]{0,2,1:T(8,128)S(1)}, f32[1536,6,64]{0,2,1:T(8,128)}, bf16[3,512,6,64]{1,3,2,0:T(8,128)(2,1)}, s32[3]{0:T(128)S(1)}, ...) while((s32[]{:T(128)}, f32[1536,6,64]{0,2,1:T(8,128)S(1)}, ...), condition=%wide.region_22.23_spmd.clone, body=%wide.region_20.22_spmd.clone.sunk | while | flops 3096968192 | bytes 245085472 | solution.py:235
  1003.8 6.8 copy-done
  1010.6 7.8 fusion.168
  1018.4 14.7 multiply_reduce_fusion.8
  1033.1 13.4 multiply_convert_fusion.6
  1061.8 6.8 copy-done
  1068.6 8.2 fusion.168
  1076.8 15.0 multiply_reduce_fusion.8
  1091.8 13.5 multiply_convert_fusion.6
  1120.4 6.8 copy-done
  1127.3 8.2 fusion.168
  1135.5 14.8 multiply_reduce_fusion.8
  1150.3 13.7 multiply_convert_fusion.6
  1180.6 5.5 copy.341
  1186.1 6.1 all-to-all-start.3
  1194.4 50.4 %all-to-all-done.3 = bf16[1536,3,1,384]{3,1,2,0:T(4,128)(2,1)} async-done(((bf16[1536,3,1,384]{3,1,2,0:T(4,128)(2,1)}), bf16[1536,3,1,384]{3,1,2,0:T(4,128)(2,1)}, u32[]{:S(2)}, u32[]{:S(2)}) %all-to-all-start.3) | async-done | bytes 3538976 | tf_op jit(solution)/shard_map/all_to_all | solution.py:247
  1251.5 7.1 convolution_convert_fusion
  1258.7 209.2 %reduce-scatter.21.cloned.1.call-done = bf16[768,4,1536]{0,2,1:T(8,128)(2,1)} async-done(((bf16[3072,4,1536]{0,2,1:T(8,128)(2,1)}), bf16[768,4,1536]{0,2,1:T(8,128)(2,1)}) %reduce-scatter.21.cloned.1.call-update) | async-done | bytes 9437200 | tf_op jit(solution)/shard_map/reduce_scatter | solution.py:177
  1471.2 7.5 fusion.73
  1479.7 21.4 %reduce-scatter.19.cloned.1.call-done = bf16[192,768]{1,0:T(8,128)(2,1)} async-done(((bf16[768,768]{1,0:T(8,128)(2,1)}), bf16[192,768]{1,0:T(8,128)(2,1)}) %reduce-scatter.19.cloned.1.call-update) | async-done | bytes 294928 | tf_op jit(solution)/shard_map/reduce_scatter | solution.py:261
  1503.0 65.4 %reduce-scatter.17.cloned.1.call-done = bf16[192,2304]{1,0:T(8,128)(2,1)} async-done(((bf16[768,2304]{1,0:T(8,128)(2,1)}), bf16[192,2304]{1,0:T(8,128)(2,1)}) %reduce-scatter.17.cloned.1.call-update) | async-done | bytes 884752 | tf_op jit(solution)/shard_map/reduce_scatter | solution.py:258
  1570.8 78.3 %reduce-scatter.23.cloned.1.call-done = bf16[768,4,192]{0,2,1:T(8,128)(2,1)} async-done(((bf16[768,4,1536]{0,2,1:T(8,128)(2,1)}), bf16[768,4,192]{0,2,1:T(8,128)(2,1)}) %reduce-scatter.23.cloned.1.call-update) | async-done | bytes 1179664 | tf_op jit(solution)/shard_map/reduce_scatter | solution.py:278
  1650.6 20.2 %reduce-scatter.29.cloned.1.call-done = bf16[192,4]{1,0:T(8,128)(2,1)} async-done(((bf16[768,4]{1,0:T(8,128)(2,1)}), bf16[192,4]{1,0:T(8,128)(2,1)}) %reduce-scatter.29.cloned.1.call-update) | async-done | bytes 1552
  1676.2 15.1 reduce-scatter.31.cloned.1.call-done
  1692.2 14.4 all-reduce.3
  1706.5 20.5 %reduce-scatter.27.cloned.1.call-done = bf16[96,192]{1,0:T(8,128)(2,1)} async-done(((bf16[768,192]{1,0:T(8,128)(2,1)}), bf16[96,192]{1,0:T(8,128)(2,1)}) %reduce-scatter.27.cloned.1.call-update) | async-done | bytes 36880
  1727.1 17.0 all_gather.31
  1745.0 23.0 %reduce-scatter.25.cloned.1.call-done = bf16[288,192]{1,0:T(8,128)(2,1)} async-done(((bf16[2304,192]{1,0:T(8,128)(2,1)}), bf16[288,192]{1,0:T(8,128)(2,1)}) %reduce-scatter.25.cloned.1.call-update) | async-done | bytes 110608
  1768.0 26.9 %all_gather.30 = bf16[192,2304]{0,1:T(8,128)(2,1)S(1)} all-gather(bf16[192,288]{0,1:T(8,128)(2,1)} %bitcast.212), channel_id=1, replica_groups=mesh['dp'=4,'seq'=2,'fsdp'=4] {'dp','seq'}, dimensions={1}, use_global_device_ids=true | all-gather | bytes 995328 | tf_op jit(solution)/shard_map/all_gather | solution.py:283
  1796.5 38.2 %all-gather.13.cloned.1.call-done = bf16[768,4,1536]{0,2,1:T(8,128)(2,1)} async-done(((bf16[768,4,192]{0,2,1:T(8,128)(2,1)}), bf16[768,4,1536]{0,2,1:T(8,128)(2,1)}) %all-gather.13.cloned.1.call-update) | async-done | bytes 9437200 | tf_op jit(solution)/shard_map/all_gather | solution.py:289
  1834.7 17.8 copy.352
  (332 shorter events, 229.1 us)
Async XLA Ops:
  7.2 75.2 %all-gather.7.cloned.1.call-start = ((), (), s32[]{:S(2)}) async-start(), calls=%async_computation.12 | async-start | bytes 4423680 | tf_op jit(solution)/shard_map/all_gather | solution.py:71
  7.9 263.5 %all-gather.9.cloned.1.call-start = ((), (), s32[]{:S(2)}) async-start(), calls=%async_computation.13 | async-start | bytes 1474560 | tf_op jit(solution)/shard_map/all_gather | solution.py:72
  8.6 735.9 %all-gather.11.cloned.1.call-start = ((), (), s32[]{:S(2)}) async-start(), calls=%async_computation.14 | async-start | bytes 47185920 | tf_op jit(solution)/shard_map/all_gather | solution.py:144
  18.0 13.8 copy-start.26
  32.4 50.0 %copy-start.12 = (bf16[1,768,768]{1,2,0:T(8,128)(2,1)}, bf16[1,768,768]{1,2,0:T(8,128)(2,1)S(1)}, u32[]{:S(2)}) copy-start(bf16[1,768,768]{1,2,0:T(8,128)(2,1)S(1)} %copy.309) | copy-start | bytes 3538948
  33.0 49.3 %copy-start.58 = (f32[768]{0:T(1024)}, f32[768]{0:T(1024)S(1)}, u32[]{:S(2)}) copy-start(f32[768]{0:T(1024)S(1)} %get-tuple-element.269) | copy-start | bytes 9220
  33.3 49.0 %copy-start.60 = (f32[768]{0:T(1024)}, f32[768]{0:T(1024)S(1)}, u32[]{:S(2)}) copy-start(f32[768]{0:T(1024)S(1)} %add_rsqrt_fusion.1) | copy-start | bytes 9220
  97.6 4.2 copy-start.38
  97.6 52.6 %all-to-all-start = ((bf16[768,3,2,384]{3,0,1,2:T(8,128)(2,1)}), bf16[768,3,2,384]{3,0,1,2:T(8,128)(2,1)S(1)}, u32[]{:S(2)}, u32[]{:S(2)}) async-start(bf16[768,3,2,384]{3,0,1,2:T(8,128)(2,1)} %copy.311), calls=%async_computation | async-start | bytes 7077888 | tf_op jit(solution)/shard_map/all_to_all | solution.py:83
  130.5 20.0 %copy-start.56 = (s32[1536]{0:T(1024)}, s32[1536]{0:T(1024)S(1)}, u32[]{:S(2)}) copy-start(s32[1536]{0:T(1024)S(1)} %fusion.98) | copy-start | bytes 18436
  153.0 4.0 copy-start.66
  221.9 13.6 copy-start.1
  221.9 13.6 copy-start.3
  221.9 13.6 copy-start.21
  246.1 5.7 copy-start.10
  247.4 19.1 %all-to-all-start.1 = ((bf16[2,2,147456]{2,1,0:T(2,128)(2,1)}), bf16[2,2,147456]{2,1,0:T(2,128)(2,1)}, u32[]{:S(2)}, u32[]{:S(2)}) async-start(bf16[2,2,147456]{2,1,0:T(2,128)(2,1)} %reshape.523), calls=%async_computation.1 | async-start | bytes 2359296 | tf_op jit(solution)/shard_map/all_to_all | solution.py:125
  251.8 1216.1 %reduce-scatter.21.cloned.1.call-start = ((), (), s32[]{:S(2)}) async-start(), calls=%async_computation.17 | async-start | bytes 47185920 | tf_op jit(solution)/shard_map/reduce_scatter | solution.py:177
  255.6 3.9 copy-start.4
  259.5 6.9 copy-start.55
  271.4 4.4 copy-start.43
  276.0 7.8 copy-start.8
  283.8 4.3 copy-start.42
  296.4 448.1 %copy-start.23 = (bf16[4,384,768]{1,2,0:T(8,128)(2,1)S(1)}, bf16[4,384,768]{1,2,0:T(8,128)(2,1)}, u32[]{:S(2)}) copy-start(bf16[4,384,768]{1,2,0:T(8,128)(2,1)} %copy.326) | copy-start | bytes 7077892
  296.4 448.1 %copy-start.63 = (pred[4,384]{1,0:T(4,128)(4,1)S(1)}, pred[4,384]{1,0:T(4,128)(4,1)}, u32[]{:S(2)}) copy-start(pred[4,384]{1,0:T(4,128)(4,1)} %gt.8) | copy-start | bytes 4612
  744.5 18.9 %copy-start.25 = (bf16[4,384,768]{1,2,0:T(8,128)(2,1)S(1)}, bf16[4,384,768]{1,2,0:T(8,128)(2,1)}, u32[]{:S(2)}) copy-start(bf16[4,384,768]{1,2,0:T(8,128)(2,1)} %copy.335) | copy-start | bytes 7077892
  884.3 6.9 copy-start.5
  955.4 3.3 copy-start.48
  955.4 3.3 copy-start.54
  955.4 3.4 copy-start.7
  955.4 3.4 copy-start.32
  955.4 3.4 copy-start.44
  955.4 3.4 copy-start.46
  955.4 3.4 copy-start.50
  958.7 4.2 copy-start.34
  958.8 4.1 copy-start.51
  958.8 4.1 copy-start.11
  958.8 4.1 copy-start.15
  966.8 19.1 %all-to-all-start.2 = ((bf16[768,2,384]{0,2,1:T(8,128)(2,1)}), bf16[768,2,384]{0,2,1:T(8,128)(2,1)S(1)}, u32[]{:S(2)}, u32[]{:S(2)}) async-start(bf16[768,2,384]{0,2,1:T(8,128)(2,1)} %bitcast.23), calls=%async_computation.2 | async-start | bytes 2359296 | tf_op jit(solution)/shard_map/all_to_all | solution.py:198
  987.0 7.5 copy-start.2
  987.0 7.5 copy-start.22
  987.0 7.5 copy-start.67
  1003.8 6.9 copy-start
  1033.1 13.4 copy-start.29
  1049.5 3.4 copy-start.30
  1061.7 6.9 copy-start
  1091.8 13.5 copy-start.29
  1108.2 3.4 copy-start.30
  1120.4 6.9 copy-start
  1150.3 13.7 copy-start.29
  1167.0 3.3 copy-start.30
  1186.1 6.1 copy-start.17
  1186.1 6.1 copy-start.28
  1186.1 58.8 %all-to-all-start.3 = ((bf16[1536,3,1,384]{3,1,2,0:T(4,128)(2,1)}), bf16[1536,3,1,384]{3,1,2,0:T(4,128)(2,1)}, u32[]{:S(2)}, u32[]{:S(2)}) async-start(bf16[1536,3,1,384]{3,1,2,0:T(4,128)(2,1)} %copy.341), calls=%async_computation.3 | async-start | bytes 9437184 | tf_op jit(solution)/shard_map/all_to_all | solution.py:247
  1192.1 308.9 %reduce-scatter.19.cloned.1.call-start = ((), (), s32[]{:S(2)}) async-start(), calls=%async_computation.16 | async-start | bytes 1474560 | tf_op jit(solution)/shard_map/reduce_scatter | solution.py:261
  1194.4 374.1 %reduce-scatter.17.cloned.1.call-start = ((), (), s32[]{:S(2)}) async-start(), calls=%async_computation.15 | async-start | bytes 4423680 | tf_op jit(solution)/shard_map/reduce_scatter | solution.py:258
  1247.7 3.7 copy-start.59
  1247.8 3.7 copy-start.61
  1258.6 390.5 %reduce-scatter.23.cloned.1.call-start = ((), (), s32[]{:S(2)}) async-start(), calls=%async_computation.18 | async-start | bytes 10616832 | tf_op jit(solution)/shard_map/reduce_scatter | solution.py:278
  1468.0 202.9 %reduce-scatter.29.cloned.1.call-start = ((), (), s32[]{:S(2)}) async-start(), calls=%async_computation.22 | async-start | bytes 245760
  1471.1 220.1 %reduce-scatter.31.cloned.1.call-start = ((), (), s32[]{:S(2)}) async-start(), calls=%async_computation.23 | async-start | bytes 245760
  1479.6 247.5 %reduce-scatter.27.cloned.1.call-start = ((), (), s32[]{:S(2)}) async-start(), calls=%async_computation.21 | async-start | bytes 442368
  1502.9 146.2 %copy-start.18 = (bf16[1,768,768]{1,2,0:T(8,128)(2,1)S(1)}, bf16[1,768,768]{1,2,0:T(8,128)(2,1)}, u32[]{:S(2)}) copy-start(bf16[1,768,768]{1,2,0:T(8,128)(2,1)} %get-tuple-element.320) | copy-start | bytes 3538948
  1502.9 265.1 %reduce-scatter.25.cloned.1.call-start = ((), (), s32[]{:S(2)}) async-start(), calls=%async_computation.20 | async-start | bytes 1327104
  1570.8 263.9 %all-gather.13.cloned.1.call-start = ((), (), s32[]{:S(2)}) async-start(), calls=%async_computation.19 | async-start | bytes 10616832 | tf_op jit(solution)/shard_map/all_gather | solution.py:289
  (26 other events, 42.1 us)
Sparse Core Ops, SparseCore 0:
  9.6 72.6 all-gather.6
  83.9 29.0 all-gather.8
  115.2 629.2 all-gather.10
  850.5 617.4 reduce-scatter.20
  1470.8 30.2 reduce-scatter.18
  1503.3 65.0 reduce-scatter.16
  1572.3 76.7 reduce-scatter.22
  1651.5 19.3 reduce-scatter.28
  1673.7 17.5 reduce-scatter.30
  1695.1 31.9 reduce-scatter.26
  1731.2 36.7 reduce-scatter.24
  1769.8 64.8 all-gather.12
where the time goes:
time: 1870 us; the launch traced here: 1860 us
  waiting for transfers between devices  1050 us (56%)
  matrix products  284 us (15%)
  local copies, waits for them, and re-layouts  251 us (13%)
  other arithmetic  143 us (8%)
  blocking collectives  83.3 us (4%)
  starting transfers between devices  18.8 us (1%)
    all_gather x1, waiting for transfers between devices, shards(): piece = lax.all_gather(expert_w, 'fsdp', axis=0, tiled=True)  444 us
    reduce_scatter x1, waiting for transfers between devices, shards(): lax.psum_scatter(jnp.concatenate([grad_first, grad_second], axis=2).astyp...  209 us
    unnamed x16, waiting for transfers between devices  80.4 us
    reduce_scatter x1, waiting for transfers between devices, shards(): lax.psum_scatter(expert_shard, ('dp', 'seq'), scatter_dimension=2, tiled=...  78.3 us
    reduce_scatter x1, waiting for transfers between devices, shards(): lax.psum_scatter(grad_qkv_w.astype(jnp.bfloat16), 'fsdp', scatter_dimensi...  65.4 us
    unnamed x149, local copies, waits for them, and re-layouts  58 us
    all_to_all x1, waiting for transfers between devices, shards(): lax.all_to_all(stacked, 'seq', split_axis=0, concat_axis=2, tiled=True)  50.4 us
    all_gather x1, waiting for transfers between devices, shards(): lax.all_gather(attn_in, 'fsdp', axis=0, tiled=True)  49 us
  transfers between devices with their start and end apart: 16, of which 13 were waited for; matrix products, arithmetic and copies ran while one was open for 28% of the time, Pallas kernels for 0%

commit v1 on v0

--- a/solution.py
+++ b/solution.py
@@ -10,6 +10,28 @@
 EPSILON = 1e-06
 NEGATIVE = -1e30
 HIGH = lax.Precision.HIGHEST
+
+
+def joined_along(tiles, dim):
+    dims = list(tiles.shape[1:])
+    dims[dim] *= tiles.shape[0]
+    return jnp.moveaxis(tiles, 0, dim).reshape(dims)
+
+
+def grow_blocks(x, axis):
+    size = lax.axis_size(axis)
+    tiles = x[None]
+    for level in range(size.bit_length() - 1):
+        bit = 1 << level
+        theirs = lax.ppermute(tiles, axis, [(i, i ^ bit) for i in range(size)])
+        both = jnp.stack([tiles, theirs])
+        upper = lax.axis_index(axis) >> level & 1
+        tiles = jnp.where(upper == 0, both, both[::-1]).reshape(-1, *x.shape)
+    return tiles
+
+
+def gather_by_bits(shard, axis, dim):
+    return joined_along(grow_blocks(shard, axis), dim)
 
 
 def route(choose, capacity, experts_count):
@@ -286,7 +308,7 @@
         lax.all_gather(part_proj.astype(jnp.bfloat16), ("dp", "seq"), axis=1, tiled=True).astype(
             part_proj.dtype
         ),
-        lax.all_gather(part_expert.astype(jnp.bfloat16), ("dp", "seq"), axis=2, tiled=True).astype(
+        gather_by_bits(part_expert.astype(jnp.bfloat16), ("dp", "seq"), 2).astype(
             part_expert.dtype
         ),
     )

time: 1870 us -> 2020 us (1.080)
  waiting for transfers between devices: 1050 us -> 1120 us
  other arithmetic: 143 us -> 178 us
  blocking collectives: 83.3 us -> 107 us
    reduce_scatter x1, waiting for transfers between devices: 209 us -> 476 us  [shards(): lax.psum_scatter(jnp.concatenate([grad_first, grad_second], axis=2).astyp...]
    reduce_scatter x1, waiting for transfers between devices: 78.3 us -> 0.02 us  [shards(): lax.psum_scatter(expert_shard, ('dp', 'seq'), scatter_dimension=2, tiled=...]
    reduce_scatter x1, waiting for transfers between devices: 65.4 us -> 11.4 us  [shards(): lax.psum_scatter(grad_qkv_w.astype(jnp.bfloat16), 'fsdp', scatter_dimensi...]
    all_gather x1 -> x0, waiting for transfers between devices: 38.2 us -> none  [shards(): lax.all_gather(part_expert.astype(jnp.bfloat16), ('dp', 'seq'), axis=2, t...]
    unnamed x16 -> x15, waiting for transfers between devices: 80.4 us -> 46.8 us
    ppermute x0 -> x3, waiting for transfers between devices: none -> 31.5 us  [grow_blocks(): theirs = lax.ppermute(tiles, axis, [(i, i ^ bit) for i in range(size)])]
    psum x1, blocking collectives: 14.4 us -> 45.8 us  [shards(): lax.psum((shard_route, shard_gains), ('dp', 'seq'))]
    reduce_scatter x1, waiting for transfers between devices: 21.4 us -> 0.02 us  [shards(): lax.psum_scatter(grad_proj_w.astype(jnp.bfloat16), 'fsdp', scatter_dimens...]
  transfers between devices with their start and end apart: 16 -> 18, of which waited for: 13 -> 11; matrix products, arithmetic and copies ran while one was open for 28% -> 27% of each run, Pallas kernels for 0% -> 0%
where the time goes in v1:
time: 2020 us; the launch traced here: 2010 us
  waiting for transfers between devices  1120 us (55%)
  matrix products  285 us (14%)
  local copies, waits for them, and re-layouts  270 us (13%)
  other arithmetic  178 us (9%)
  blocking collectives  107 us (5%)
  starting transfers between devices  21 us (1%)
    reduce_scatter x1, waiting for transfers between devices, shards(): lax.psum_scatter(jnp.concatenate([grad_first, grad_second], axis=2).astyp...  476 us
    all_gather x1, waiting for transfers between devices, shards(): piece = lax.all_gather(expert_w, 'fsdp', axis=0, tiled=True)  444 us
    unnamed x147, local copies, waits for them, and re-layouts  63.7 us
    all_to_all x1, waiting for transfers between devices, shards(): lax.all_to_all(stacked, 'seq', split_axis=0, concat_axis=2, tiled=True)  50.9 us
    all_gather x1, waiting for transfers between devices, shards(): lax.all_gather(attn_in, 'fsdp', axis=0, tiled=True)  49 us
    unnamed x15, waiting for transfers between devices  46.8 us
    psum x1, blocking collectives, shards(): lax.psum((shard_route, shard_gains), ('dp', 'seq'))  45.8 us
    dot_general x3, matrix products, back_block(): jnp.einsum('qhd,khd->hqk', grad_block, values, preferred_element_type=jnp...  45 us
  transfers between devices with their start and end apart: 18, of which 11 were waited for; matrix products, arithmetic and copies ran while one was open for 27% of the time, Pallas kernels for 0%

profile of v1, /device:TPU:0, one launch (start us, length us, event | category | flops | bytes accessed | tf_op | source)
XLA Modules:
  0.0 2013.1 jit_solution(11664779237122675888)
XLA Ops:
  8.7 9.3 copy.334
  18.7 13.0 all-gather
  33.3 49.0 %all-gather.6.cloned.1.call-done = bf16[768,2304]{1,0:T(8,128)(2,1)} async-done(((bf16[192,2304]{1,0:T(8,128)(2,1)}), bf16[768,2304]{1,0:T(8,128)(2,1)}) %all-gather.6.cloned.1.call-update) | async-done | bytes 3538960 | tf_op jit(solution)/shard_map/all_gather | solution.py:93
  82.3 6.6 convolution_convert_fusion.1
  88.9 6.5 reshape.450
  105.7 12.0 all-gather.1
  130.6 6.7 scatter_custom_fusion.1
  137.9 6.8 scatter_custom_fusion
  157.0 65.0 %while.28 = (s32[]{:T(128)}, bf16[3,512,6,64]{1,3,2,0:T(8,128)(2,1)}, f32[3,6,512]{2,1,0:T(8,128)}, s32[3]{0:T(128)S(1)}, s32[1536]{0:T(1024)S(1)}, /*index=5*/b...) while((s32[]{:T(128)}, ...), condition=%wide.region_4.5_spmd.clone, body=%wide.region_1.4_spmd.clone.sunk | while | flops 1267923968 | bytes 63042744 | solution.py:145
  170.9 7.1 fusion.158
  192.6 7.1 fusion.158
  214.2 7.1 fusion.158
  221.9 5.0 copy.365
  226.9 8.6 reshape.522
  236.0 10.1 reduce.12
  259.5 6.9 mul.305
  278.1 5.7 gather_fusion
  290.8 5.6 gather_fusion.2
  300.9 443.7 %all-gather.10.cloned.1.call-done = bf16[3072,4,1536]{2,0,1:T(8,128)(2,1)} async-done(((bf16[768,4,1536]{2,0,1:T(8,128)(2,1)}), bf16[3072,4,1536]{2,0,1:T(8,128)(2,1)}) %all-gather.10.cloned.1.call-update) | async-done | bytes 37748752 | tf_op jit(solution)/shard_map/all_gather | solution.py:166
  744.5 18.9 fusion.56
  763.4 19.1 convert_bitcast_fusion
  782.5 25.0 %fusion.49 = bf16[4,384,3072]{2,1,0:T(8,128)(2,1)} fusion(f32[4,384,3072]{2,1,0:T(8,128)} %fusion.56, bf16[3072,4,1536]{2,0,1:T(8,128)(2,1)} %all-gather.10.cloned.1.call-done, bf16[4,384,768]{1,2,0:T(8,128)(2,1)} %copy.342, pred[4,384]{1,0:T(4,128)(4,1)S(1)} %copy-done.62), kind=kOutput, calls=%fused_computation.67 | convolution fusion | flops 7343308800 | bytes 49546752 | tf_op jit(solution)/shard_map/ecd,fed->ecf/dot_general | solution.py:76
  807.5 17.0 convert_bitcast_fusion.1
  824.5 25.8 %pad_maximum_fusion = bf16[3072,4,1536]{0,2,1:T(8,128)(2,1)} fusion(bf16[3072,4,768]{0,2,1:T(8,128)(2,1)} %convert_bitcast_fusion, bf16[3072,4,768]{0,2,1:T(8,128)(2,1)} %convert_bitcast_fusion.1), kind=kLoop, calls=%fused_computation.58 | loop fusion | flops 75497472 | bytes 75497472 | tf_op jit(solution)/shard_map/concatenate | solution.py:200
  851.8 18.4 fusion.52
  875.2 9.1 gather_fusion.1
  884.3 6.9 reshape.455
  891.2 13.5 multiply_reduce_fusion.1
  908.0 17.1 fusion.54
  929.9 9.1 gather_fusion.3
  939.0 6.9 reshape.457
  945.9 9.4 reduce_sum.159
  970.5 15.5 all-to-all-done.2
  992.1 475.8 %reduce-scatter.21.cloned.1.call-done = bf16[768,4,1536]{0,2,1:T(8,128)(2,1)} async-done(((bf16[3072,4,1536]{0,2,1:T(8,128)(2,1)}), bf16[768,4,1536]{0,2,1:T(8,128)(2,1)}) %reduce-scatter.21.cloned.1.call-update) | async-done | bytes 9437200 | tf_op jit(solution)/shard_map/reduce_scatter | solution.py:199
  1469.2 179.4 %while.29 = (s32[]{:T(128)}, f32[1536,6,64]{0,2,1:T(8,128)S(1)}, f32[1536,6,64]{0,2,1:T(8,128)}, bf16[3,512,6,64]{1,3,2,0:T(8,128)(2,1)}, s32[3]{0:T(128)S(1)}, ...) while((s32[]{:T(128)}, f32[1536,6,64]{0,2,1:T(8,128)S(1)}, ...), condition=%wide.region_22.23_spmd.clone, body=%wide.region_20.22_spmd.clone.sunk | while | flops 3096968192 | bytes 245085472 | solution.py:257
  1478.4 9.9 copy-done
  1488.2 7.8 fusion.171
  1496.0 15.5 multiply_reduce_fusion.8
  1511.5 13.9 multiply_convert_fusion.6
  1540.6 6.8 copy-done
  1547.5 8.2 fusion.171
  1555.7 14.8 multiply_reduce_fusion.8
  1570.5 13.3 multiply_convert_fusion.6
  1599.0 6.8 copy-done
  1605.9 8.2 fusion.171
  1614.0 14.8 multiply_reduce_fusion.8
  1628.8 13.3 multiply_convert_fusion.6
  1658.7 5.5 copy.348
  1664.2 6.1 all-to-all-start.3
  1672.6 50.9 %all-to-all-done.3 = bf16[1536,3,1,384]{3,1,2,0:T(4,128)(2,1)} async-done(((bf16[1536,3,1,384]{3,1,2,0:T(4,128)(2,1)}), bf16[1536,3,1,384]{3,1,2,0:T(4,128)(2,1)}, u32[]{:S(2)}, u32[]{:S(2)}) %all-to-all-start.3) | async-done | bytes 3538976 | tf_op jit(solution)/shard_map/all_to_all | solution.py:269
  1730.0 7.1 convolution_convert_fusion
  1737.6 26.6 %collective-permute-done = bf16[1,768,4,192]{1,3,2,0:T(8,128)(2,1)S(1)} collective-permute-done((bf16[1,768,4,192]{1,3,2,0:T(8,128)(2,1)}, bf16[1,768,4,192]{1,3,2,0:T(8,128)(2,1)S(1)}, u32[]{:S(2)}, u32[]{:S(2)}) %collective-permute-start) | collective-permute-done | bytes 1179680 | tf_op jit(solution)/shard_map/ppermute | solution.py:26
  1781.9 7.7 fusion.74
  1792.6 11.4 reduce-scatter.17.cloned.1.call-done
  1808.8 17.9 reduce-scatter.29.cloned.1.call-done
  1833.2 13.3 reduce-scatter.31.cloned.1.call-done
  1847.3 45.8 %all-reduce.3 = (f32[192,4]{0,1:T(4,128)}, f32[192,2]{0,1:T(2,128)}) all-reduce(bf16[192,4]{0,1:T(4,128)(2,1)S(1)} %copy.371, bf16[192,2]{0,1:T(2,128)(2,1)S(1)} %copy.373), channel_id=1, replica_groups=mesh['dp'=4,'seq'=2,'fsdp'=4] {'dp','seq'}, use_global_device_ids=true, to_apply=%region_29.30 | all-reduce | flops 1152 | bytes 6912 | tf_op jit(solution)/shard_map/psum | solution.py:315
  1893.1 15.7 all_gather.28
  1909.8 14.1 reduce-scatter.25.cloned.1.call-done
  1923.9 20.6 %all_gather.27 = bf16[192,2304]{0,1:T(8,128)(2,1)S(1)} all-gather(bf16[192,288]{0,1:T(8,128)(2,1)} %bitcast.232), channel_id=1, replica_groups=mesh['dp'=4,'seq'=2,'fsdp'=4] {'dp','seq'}, dimensions={1}, use_global_device_ids=true | all-gather | bytes 995328 | tf_op jit(solution)/shard_map/all_gather | solution.py:305
  1946.1 8.3 pad_maximum_fusion.1
  1954.4 16.8 fusion.58
  1971.2 12.6 copy.355
  1983.8 22.6 %copy.360 = f32[768,4,1536]{2,1,0:T(4,128)} copy(f32[768,4,1536]{0,2,1:T(8,128)} %bitcast.210) | data formatting | bytes 37748736
  (340 shorter events, 245.0 us)
Async XLA Ops:
  7.2 75.2 %all-gather.6.cloned.1.call-start = ((), (), s32[]{:S(2)}) async-start(), calls=%async_computation.12 | async-start | bytes 4423680 | tf_op jit(solution)/shard_map/all_gather | solution.py:93
  7.9 263.5 %all-gather.8.cloned.1.call-start = ((), (), s32[]{:S(2)}) async-start(), calls=%async_computation.13 | async-start | bytes 1474560 | tf_op jit(solution)/shard_map/all_gather | solution.py:94
  8.6 735.9 %all-gather.10.cloned.1.call-start = ((), (), s32[]{:S(2)}) async-start(), calls=%async_computation.14 | async-start | bytes 47185920 | tf_op jit(solution)/shard_map/all_gather | solution.py:166
  18.0 13.8 copy-start.25
  32.4 50.0 %copy-start.12 = (bf16[1,768,768]{1,2,0:T(8,128)(2,1)}, bf16[1,768,768]{1,2,0:T(8,128)(2,1)S(1)}, u32[]{:S(2)}) copy-start(bf16[1,768,768]{1,2,0:T(8,128)(2,1)S(1)} %copy.316) | copy-start | bytes 3538948
  33.0 49.3 %copy-start.57 = (f32[768]{0:T(1024)}, f32[768]{0:T(1024)S(1)}, u32[]{:S(2)}) copy-start(f32[768]{0:T(1024)S(1)} %get-tuple-element.269) | copy-start | bytes 9220
  33.3 49.0 %copy-start.59 = (f32[768]{0:T(1024)}, f32[768]{0:T(1024)S(1)}, u32[]{:S(2)}) copy-start(f32[768]{0:T(1024)S(1)} %add_rsqrt_fusion.1) | copy-start | bytes 9220
  97.6 4.2 copy-start.37
  97.6 52.6 %all-to-all-start = ((bf16[768,3,2,384]{3,0,1,2:T(8,128)(2,1)}), bf16[768,3,2,384]{3,0,1,2:T(8,128)(2,1)S(1)}, u32[]{:S(2)}, u32[]{:S(2)}) async-start(bf16[768,3,2,384]{3,0,1,2:T(8,128)(2,1)} %copy.318), calls=%async_computation | async-start | bytes 7077888 | tf_op jit(solution)/shard_map/all_to_all | solution.py:105
  130.5 20.0 copy-start.55
  153.0 4.0 copy-start.65
  221.9 13.6 copy-start.1
  221.9 13.6 copy-start.3
  221.9 13.6 copy-start.20
  246.1 5.7 copy-start.10
  247.4 19.1 all-to-all-start.1
  251.8 1216.1 %reduce-scatter.21.cloned.1.call-start = ((), (), s32[]{:S(2)}) async-start(), calls=%async_computation.17 | async-start | bytes 47185920 | tf_op jit(solution)/shard_map/reduce_scatter | solution.py:199
  255.6 3.9 copy-start.4
  259.5 6.9 copy-start.54
  271.4 4.4 copy-start.42
  276.0 7.8 copy-start.8
  283.8 4.3 copy-start.41
  296.4 448.1 %copy-start.23 = (bf16[4,384,768]{1,2,0:T(8,128)(2,1)S(1)}, bf16[4,384,768]{1,2,0:T(8,128)(2,1)}, u32[]{:S(2)}) copy-start(bf16[4,384,768]{1,2,0:T(8,128)(2,1)} %copy.333) | copy-start | bytes 7077892
  296.4 448.1 %copy-start.62 = (pred[4,384]{1,0:T(4,128)(4,1)S(1)}, pred[4,384]{1,0:T(4,128)(4,1)}, u32[]{:S(2)}) copy-start(pred[4,384]{1,0:T(4,128)(4,1)} %gt.8) | copy-start | bytes 4612
  744.5 18.9 copy-start.24
  884.3 6.9 copy-start.5
  955.4 3.4 copy-start.31
  955.4 3.4 copy-start.43
  955.4 3.4 copy-start.45
  958.7 4.2 copy-start.33
  958.8 4.1 copy-start.50
  958.8 4.1 copy-start.11
  958.8 4.1 copy-start.15
  966.8 19.1 all-to-all-start.2
  970.4 766.8 %reduce-scatter.23.cloned.1.call-start = ((), (), s32[]{:S(2)}) async-start(), calls=%async_computation.18 | async-start | bytes 10616832 | tf_op jit(solution)/shard_map/reduce_scatter | solution.py:300
  1478.3 9.9 copy-start
  1511.5 13.9 copy-start.28
  1528.4 3.4 copy-start.29
  1540.6 6.9 copy-start
  1570.5 13.3 copy-start.28
  1586.8 3.4 copy-start.29
  1599.0 6.9 copy-start
  1628.8 13.3 copy-start.28
  1664.2 6.1 copy-start.17
  1664.2 6.1 copy-start.27
  1664.2 59.2 %all-to-all-start.3 = ((bf16[1536,3,1,384]{3,1,2,0:T(4,128)(2,1)}), bf16[1536,3,1,384]{3,1,2,0:T(4,128)(2,1)}, u32[]{:S(2)}, u32[]{:S(2)}) async-start(bf16[1536,3,1,384]{3,1,2,0:T(4,128)(2,1)} %copy.348), calls=%async_computation.3 | async-start | bytes 9437184 | tf_op jit(solution)/shard_map/all_to_all | solution.py:269
  1670.3 120.3 %reduce-scatter.19.cloned.1.call-start = ((), (), s32[]{:S(2)}) async-start(), calls=%async_computation.16 | async-start | bytes 1474560 | tf_op jit(solution)/shard_map/reduce_scatter | solution.py:283
  1672.5 131.5 %reduce-scatter.17.cloned.1.call-start = ((), (), s32[]{:S(2)}) async-start(), calls=%async_computation.15 | async-start | bytes 4423680 | tf_op jit(solution)/shard_map/reduce_scatter | solution.py:280
  1726.2 3.7 copy-start.58
  1726.3 3.7 copy-start.60
  1737.1 89.5 %reduce-scatter.29.cloned.1.call-start = ((), (), s32[]{:S(2)}) async-start(), calls=%async_computation.21 | async-start | bytes 245760
  1737.2 26.9 %collective-permute-start = (bf16[1,768,4,192]{1,3,2,0:T(8,128)(2,1)}, bf16[1,768,4,192]{1,3,2,0:T(8,128)(2,1)S(1)}, u32[]{:S(2)}, u32[]{:S(2)}) collective-permute-start(bf16[1,768,4,192]{1,3,2,0:T(8,128)(2,1)} %bitcast.229), channel_id=1, source_target_pairs={{0,4},{4,0},{8,12},{12,8},{16,20},{20,16},{24,28},{28,24},{1,5},{5... | collective-permute-start | bytes 3538952 | tf_op jit(solution)/shard_map/ppermute | solution.py:26
  1767.7 4.9 collective-permute-start.1
  1774.7 5.0 copy-start.9
  1774.7 5.0 copy-start.32
  1774.8 5.0 copy-start.34
  1774.8 5.0 copy-start.51
  1774.8 6.9 copy-start.61
  1774.8 7.1 copy-start.14
  1778.1 168.0 %collective-permute-start.2 = (bf16[4,768,4,192]{1,3,2,0:T(8,128)(2,1)}, bf16[4,768,4,192]{1,3,2,0:T(8,128)(2,1)}, u32[]{:S(2)}, u32[]{:S(2)}) collective-permute-start(bf16[4,768,4,192]{1,3,2,0:T(8,128)(2,1)} %bitcast.42), channel_id=1, source_target_pairs={{0,16},{4,20},{8,24},{12,28},{16,0},{20,4},{24,8},{28,12},{1,17},{... | collective-permute-start | bytes 14155784 | tf_op jit(solution)/shard_map/ppermute | solution.py:26
  1781.7 64.8 %reduce-scatter.31.cloned.1.call-start = ((), (), s32[]{:S(2)}) async-start(), calls=%async_computation.22 | async-start | bytes 245760
  1790.5 102.6 %reduce-scatter.27.cloned.1.call-start = ((), (), s32[]{:S(2)}) async-start(), calls=%async_computation.20 | async-start | bytes 442368
  1792.5 35.0 %copy-start.18 = (f32[768,768]{0,1:T(8,128)S(1)}, f32[768,768]{0,1:T(8,128)}, u32[]{:S(2)}) copy-start(f32[768,768]{0,1:T(8,128)} %copy-done.16) | copy-start | bytes 7077892
  1792.5 131.4 %reduce-scatter.25.cloned.1.call-start = ((), (), s32[]{:S(2)}) async-start(), calls=%async_computation.19 | async-start | bytes 1327104
  (27 other events, 50.1 us)
Sparse Core Ops, SparseCore 0:
  9.6 72.6 all-gather.5
  83.9 29.0 all-gather.7
  115.2 629.2 all-gather.9
  850.5 617.4 reduce-scatter.20
  1471.7 77.5 reduce-scatter.22
  1673.8 30.7 reduce-scatter.18
  1737.3 66.7 reduce-scatter.16
  1806.9 19.6 reduce-scatter.28
  1828.9 17.5 reduce-scatter.30
  1850.2 32.8 reduce-scatter.26
  1886.7 37.1 reduce-scatter.24
